TPU v7x, 256 devices: a whole 4x4x8 slice. The times are simulated.
256 devices in a mesh: row: 16 (over z_hi, y, core), col: 16 (over x, z_lo).
Axes of the slice: x: 4, y: 4, z: 8 (z_hi: 2, z_lo: 4; z = z_hi * 4 + z_lo), core: 2. Of those that a mesh axis runs over, the one named last changes fastest.
Arguments:
- act_sketch: bfloat16 [2, 8192, 256], P(None, 'row'), may hold values from -6 to 6
- grad_sketch: bfloat16 [2, 8192, 256], P(None, 'row'), may hold values from -6 to 6
- targets: float32 [8192, 256], P('row'), may hold values from -6 to 6
Outputs:
- residual: float32 [8192, 256], P(('row', 'col'))
All inputs are finite; a program needn't handle non-finite values.
Results may differ from a plain program's by a relative error of at most 0.014.
The roundings to bfloat16 on the way count: a program that leaves them out, or rounds other values in their place, can miss the bound.
Values may be sent and summed in bfloat16 or wider, within the bound.
A program may use at most 64 MiB of HBM per device.

v0:
```python
import math
import jax
import jax.numpy as jnp
from jax import lax
from jax.sharding import PartitionSpec as P

ITERS = 8


def broadcast(value, axis, source):
    kept = jnp.where(lax.axis_index(axis) == source, value, 0).astype(value.dtype)
    return lax.psum(kept, axis)


def spread(panel, root):
    return broadcast(panel, "row", root)


def gram_pair(left, right):
    return lax.dot_general(
        left, right, (((1,), (1,)), ((), ())), preferred_element_type=jnp.float32
    )


def body(act_sketch, grad_sketch, targets):
    row_count = lax.axis_size("row")
    col_count = lax.axis_size("col")
    ratio = col_count // row_count
    examples = targets.shape[0]
    col_block = examples // ratio
    share_rows = examples // col_count
    col_place = lax.axis_index("col")
    root = col_place // ratio
    scale = act_sketch.shape[2] * math.sqrt(examples * row_count) / 4.0
    act_cols, grad_cols = (broadcast(act_sketch, "row", root), broadcast(grad_sketch, "row", root))
    total = jnp.zeros((examples, col_block), jnp.float32)
    for layer in range(act_sketch.shape[0]):
        act_gram = gram_pair(act_sketch[layer], act_cols[layer])
        grad_gram = gram_pair(grad_sketch[layer], grad_cols[layer])
        total = total + act_gram * grad_gram
    kernel = (total / scale).astype(jnp.bfloat16)
    share = lax.dynamic_slice_in_dim(targets, col_place * share_rows, share_rows, 0)
    for step in range(ITERS):
        squashed = jnp.tanh(share).astype(jnp.bfloat16)
        gathered = lax.all_gather(squashed, "col", axis=0, tiled=True)
        panel = spread(gathered, root)
        partial_value = jnp.dot(kernel, panel, preferred_element_type=jnp.float32)
        piece = lax.psum_scatter(partial_value, "col", scatter_dimension=0, tiled=True)
        share = share - 0.05 * piece
    return share


def solution(mesh):
    return jax.shard_map(
        body,
        mesh=mesh,
        in_specs=(P(None, "row", None), P(None, "row", None), P("row", None)),
        out_specs=P(("row", "col"), None),
        check_vma=False,
    )
```

profile of v0, /device:TPU:8, one launch (start us, length us, event | category | flops | bytes accessed | tf_op | source)
XLA Modules:
  0.0 2479.9 jit_solution(18417355909062240451)
XLA Ops:
  7.4 46.0 %all_gather.24 = bf16[512,256]{1,0:T(8,128)(2,1)S(1)} all-gather(bf16[32,256]{1,0:T(8,128)(2,1)S(1)} %tanh_convert_fusion.7), channel_id=1, replica_groups=mesh['row'=16,'col'=16] {'col'}, dimensions={0}, use_global_device_ids=true | all-gather | bytes 278528 | tf_op jit(solution)/shard_map/all_gather | solution.py:45
  55.2 172.0 %all-reduce.24.cloned.1.call-done = (bf16[2,512,256]{2,1,0:T(8,128)(2,1)}, bf16[2,512,256]{2,1,0:T(8,128)(2,1)}, bf16[512,256]{1,0:T(8,128)(2,1)}) async-done(((bf16[2,512,256]{2,1,0:T(8,128)(2,1)}, bf16[2,512,256]{2,1,0:T(8,128)(2,1)}, bf16[512,256]{1,0:T(8,128)(2,1)}), (bf16[2,512,256]{2,1,0:T(8,128)(2,1)}, bf16[2,512,256]{2,1,0:T(8,128)(2,1)}, bf16[512,256]{1,0:T(8,128)(2,1)})) %all-reduce.24.cloned.1.call-update) | async-done | bytes 1310736 | tf_op jit(solution)/shard_map/psum | solution.py:12
  232.1 94.1 %reduce-scatter.9.cloned.1.call-done = f32[32,256]{1,0:T(8,128)} async-done(((f32[512,256]{1,0:T(8,128)}), f32[32,256]{1,0:T(8,128)}) %reduce-scatter.9.cloned.1.call-update) | async-done | bytes 32784 | tf_op jit(solution)/shard_map/reduce_scatter | solution.py:48
  327.0 39.1 %all_gather.25 = bf16[512,256]{1,0:T(8,128)(2,1)S(1)} all-gather(bf16[32,256]{1,0:T(8,128)(2,1)S(1)} %get-tuple-element.12), channel_id=1, replica_groups=mesh['row'=16,'col'=16] {'col'}, dimensions={0}, use_global_device_ids=true | all-gather | bytes 278528 | tf_op jit(solution)/shard_map/all_gather | solution.py:45
  367.0 169.6 %all-reduce.10.cloned.1.call-done = bf16[512,256]{1,0:T(8,128)(2,1)} async-done(((bf16[512,256]{1,0:T(8,128)(2,1)}), bf16[512,256]{1,0:T(8,128)(2,1)}) %all-reduce.10.cloned.1.call-update) | async-done | bytes 262160 | tf_op jit(solution)/shard_map/psum | solution.py:12
  536.6 2.1 fusion.14
  538.7 94.2 %reduce-scatter.11.cloned.1.call-done = f32[32,256]{1,0:T(8,128)} async-done(((f32[512,256]{1,0:T(8,128)}), f32[32,256]{1,0:T(8,128)}) %reduce-scatter.11.cloned.1.call-update) | async-done | bytes 32784 | tf_op jit(solution)/shard_map/reduce_scatter | solution.py:48
  633.8 39.5 %all_gather.26 = bf16[512,256]{1,0:T(8,128)(2,1)S(1)} all-gather(bf16[32,256]{1,0:T(8,128)(2,1)S(1)} %tanh_convert_fusion.5), channel_id=1, replica_groups=mesh['row'=16,'col'=16] {'col'}, dimensions={0}, use_global_device_ids=true | all-gather | bytes 278528 | tf_op jit(solution)/shard_map/all_gather | solution.py:45
  674.0 169.0 %all-reduce.12.cloned.1.call-done = bf16[512,256]{1,0:T(8,128)(2,1)} async-done(((bf16[512,256]{1,0:T(8,128)(2,1)}), bf16[512,256]{1,0:T(8,128)(2,1)}) %all-reduce.12.cloned.1.call-update) | async-done | bytes 262160 | tf_op jit(solution)/shard_map/psum | solution.py:12
  843.0 2.1 fusion.15
  845.2 94.2 %reduce-scatter.13.cloned.1.call-done = f32[32,256]{1,0:T(8,128)} async-done(((f32[512,256]{1,0:T(8,128)}), f32[32,256]{1,0:T(8,128)}) %reduce-scatter.13.cloned.1.call-update) | async-done | bytes 32784 | tf_op jit(solution)/shard_map/reduce_scatter | solution.py:48
  940.2 39.5 %all_gather.27 = bf16[512,256]{1,0:T(8,128)(2,1)S(1)} all-gather(bf16[32,256]{1,0:T(8,128)(2,1)S(1)} %get-tuple-element.10), channel_id=1, replica_groups=mesh['row'=16,'col'=16] {'col'}, dimensions={0}, use_global_device_ids=true | all-gather | bytes 278528 | tf_op jit(solution)/shard_map/all_gather | solution.py:45
  980.5 169.0 %all-reduce.14.cloned.1.call-done = bf16[512,256]{1,0:T(8,128)(2,1)} async-done(((bf16[512,256]{1,0:T(8,128)(2,1)}), bf16[512,256]{1,0:T(8,128)(2,1)}) %all-reduce.14.cloned.1.call-update) | async-done | bytes 262160 | tf_op jit(solution)/shard_map/psum | solution.py:12
  1149.5 2.1 fusion.16
  1151.6 94.4 %reduce-scatter.15.cloned.1.call-done = f32[32,256]{1,0:T(8,128)} async-done(((f32[512,256]{1,0:T(8,128)}), f32[32,256]{1,0:T(8,128)}) %reduce-scatter.15.cloned.1.call-update) | async-done | bytes 32784 | tf_op jit(solution)/shard_map/reduce_scatter | solution.py:48
  1246.8 39.5 %all_gather.28 = bf16[512,256]{1,0:T(8,128)(2,1)S(1)} all-gather(bf16[32,256]{1,0:T(8,128)(2,1)S(1)} %tanh_convert_fusion.3), channel_id=1, replica_groups=mesh['row'=16,'col'=16] {'col'}, dimensions={0}, use_global_device_ids=true | all-gather | bytes 278528 | tf_op jit(solution)/shard_map/all_gather | solution.py:45
  1287.1 169.2 %all-reduce.16.cloned.1.call-done = bf16[512,256]{1,0:T(8,128)(2,1)} async-done(((bf16[512,256]{1,0:T(8,128)(2,1)}), bf16[512,256]{1,0:T(8,128)(2,1)}) %all-reduce.16.cloned.1.call-update) | async-done | bytes 262160 | tf_op jit(solution)/shard_map/psum | solution.py:12
  1456.3 2.1 fusion.17
  1458.5 94.2 %reduce-scatter.17.cloned.1.call-done = f32[32,256]{1,0:T(8,128)} async-done(((f32[512,256]{1,0:T(8,128)}), f32[32,256]{1,0:T(8,128)}) %reduce-scatter.17.cloned.1.call-update) | async-done | bytes 32784 | tf_op jit(solution)/shard_map/reduce_scatter | solution.py:48
  1553.5 39.5 %all_gather.29 = bf16[512,256]{1,0:T(8,128)(2,1)S(1)} all-gather(bf16[32,256]{1,0:T(8,128)(2,1)S(1)} %get-tuple-element.8), channel_id=1, replica_groups=mesh['row'=16,'col'=16] {'col'}, dimensions={0}, use_global_device_ids=true | all-gather | bytes 278528 | tf_op jit(solution)/shard_map/all_gather | solution.py:45
  1593.7 169.0 %all-reduce.18.cloned.1.call-done = bf16[512,256]{1,0:T(8,128)(2,1)} async-done(((bf16[512,256]{1,0:T(8,128)(2,1)}), bf16[512,256]{1,0:T(8,128)(2,1)}) %all-reduce.18.cloned.1.call-update) | async-done | bytes 262160 | tf_op jit(solution)/shard_map/psum | solution.py:12
  1762.8 2.1 fusion.18
  1764.9 94.2 %reduce-scatter.19.cloned.1.call-done = f32[32,256]{1,0:T(8,128)} async-done(((f32[512,256]{1,0:T(8,128)}), f32[32,256]{1,0:T(8,128)}) %reduce-scatter.19.cloned.1.call-update) | async-done | bytes 32784 | tf_op jit(solution)/shard_map/reduce_scatter | solution.py:48
  1859.9 39.5 %all_gather.30 = bf16[512,256]{1,0:T(8,128)(2,1)S(1)} all-gather(bf16[32,256]{1,0:T(8,128)(2,1)S(1)} %tanh_convert_fusion.1), channel_id=1, replica_groups=mesh['row'=16,'col'=16] {'col'}, dimensions={0}, use_global_device_ids=true | all-gather | bytes 278528 | tf_op jit(solution)/shard_map/all_gather | solution.py:45
  1900.2 169.0 %all-reduce.20.cloned.1.call-done = bf16[512,256]{1,0:T(8,128)(2,1)} async-done(((bf16[512,256]{1,0:T(8,128)(2,1)}), bf16[512,256]{1,0:T(8,128)(2,1)}) %all-reduce.20.cloned.1.call-update) | async-done | bytes 262160 | tf_op jit(solution)/shard_map/psum | solution.py:12
  2069.2 2.1 fusion.19
  2071.4 94.2 %reduce-scatter.21.cloned.1.call-done = f32[32,256]{1,0:T(8,128)} async-done(((f32[512,256]{1,0:T(8,128)}), f32[32,256]{1,0:T(8,128)}) %reduce-scatter.21.cloned.1.call-update) | async-done | bytes 32784 | tf_op jit(solution)/shard_map/reduce_scatter | solution.py:48
  2166.4 39.5 %all_gather.31 = bf16[512,256]{1,0:T(8,128)(2,1)S(1)} all-gather(bf16[32,256]{1,0:T(8,128)(2,1)S(1)} %tanh_convert_fusion), channel_id=1, replica_groups=mesh['row'=16,'col'=16] {'col'}, dimensions={0}, use_global_device_ids=true | all-gather | bytes 278528 | tf_op jit(solution)/shard_map/all_gather | solution.py:45
  2206.6 169.0 %all-reduce.22.cloned.1.call-done = bf16[512,256]{1,0:T(8,128)(2,1)} async-done(((bf16[512,256]{1,0:T(8,128)(2,1)}), bf16[512,256]{1,0:T(8,128)(2,1)}) %all-reduce.22.cloned.1.call-update) | async-done | bytes 262160 | tf_op jit(solution)/shard_map/psum | solution.py:12
  2375.7 2.1 fusion.20
  2377.8 94.2 %reduce-scatter.23.cloned.1.call-done = f32[32,256]{1,0:T(8,128)} async-done(((f32[512,256]{1,0:T(8,128)}), f32[32,256]{1,0:T(8,128)}) %reduce-scatter.23.cloned.1.call-update) | async-done | bytes 32784 | tf_op jit(solution)/shard_map/reduce_scatter | solution.py:48
  2472.0 1.4 multiply_subtract_fusion
  (72 shorter events, 18.8 us)
Async XLA Ops:
  6.5 47.5 %copy-start = (bf16[2,512,256]{2,1,0:T(8,128)(2,1)S(1)}, bf16[2,512,256]{2,1,0:T(8,128)(2,1)}, u32[]{:S(2)}) copy-start(bf16[2,512,256]{2,1,0:T(8,128)(2,1)} %param.4) | copy-start | bytes 1572868
  6.5 220.7 %all-reduce.24.cloned.1.call-start = ((), (), s32[]{:S(2)}) async-start(), calls=%async_computation.23 | async-start | bytes 2621440 | tf_op jit(solution)/shard_map/psum | solution.py:12
  55.1 172.1 %copy-start.1 = (bf16[2,512,256]{2,1,0:T(8,128)(2,1)S(1)}, bf16[2,512,256]{2,1,0:T(8,128)(2,1)}, u32[]{:S(2)}) copy-start(bf16[2,512,256]{2,1,0:T(8,128)(2,1)} %param.3) | copy-start | bytes 1572868
  55.1 271.1 %reduce-scatter.9.cloned.1.call-start = ((), (), s32[]{:S(2)}) async-start(), calls=%async_computation.8 | async-start | bytes 557056 | tf_op jit(solution)/shard_map/reduce_scatter | solution.py:48
  227.2 1.4 copy-start.3
  228.6 1.0 copy-start.2
  230.0 1.0 copy-start.5
  232.1 304.5 %all-reduce.10.cloned.1.call-start = ((), (), s32[]{:S(2)}) async-start(), calls=%async_computation.9 | async-start | bytes 524288 | tf_op jit(solution)/shard_map/psum | solution.py:12
  366.9 266.1 %reduce-scatter.11.cloned.1.call-start = ((), (), s32[]{:S(2)}) async-start(), calls=%async_computation.10 | async-start | bytes 557056 | tf_op jit(solution)/shard_map/reduce_scatter | solution.py:48
  538.7 304.3 %all-reduce.12.cloned.1.call-start = ((), (), s32[]{:S(2)}) async-start(), calls=%async_computation.11 | async-start | bytes 524288 | tf_op jit(solution)/shard_map/psum | solution.py:12
  674.0 265.5 %reduce-scatter.13.cloned.1.call-start = ((), (), s32[]{:S(2)}) async-start(), calls=%async_computation.12 | async-start | bytes 557056 | tf_op jit(solution)/shard_map/reduce_scatter | solution.py:48
  845.1 94.3 %copy-start.7 = (f32[32,256]{1,0:T(8,128)S(1)}, f32[32,256]{1,0:T(8,128)}, u32[]{:S(2)}) copy-start(f32[32,256]{1,0:T(8,128)} %reduce-scatter.11.cloned.1.call-done) | copy-start | bytes 98308
  845.1 304.4 %all-reduce.14.cloned.1.call-start = ((), (), s32[]{:S(2)}) async-start(), calls=%async_computation.13 | async-start | bytes 524288 | tf_op jit(solution)/shard_map/psum | solution.py:12
  980.4 265.6 %reduce-scatter.15.cloned.1.call-start = ((), (), s32[]{:S(2)}) async-start(), calls=%async_computation.14 | async-start | bytes 557056 | tf_op jit(solution)/shard_map/reduce_scatter | solution.py:48
  1151.6 304.7 %all-reduce.16.cloned.1.call-start = ((), (), s32[]{:S(2)}) async-start(), calls=%async_computation.15 | async-start | bytes 524288 | tf_op jit(solution)/shard_map/psum | solution.py:12
  1287.1 265.7 %reduce-scatter.17.cloned.1.call-start = ((), (), s32[]{:S(2)}) async-start(), calls=%async_computation.16 | async-start | bytes 557056 | tf_op jit(solution)/shard_map/reduce_scatter | solution.py:48
  1458.4 94.3 %copy-start.8 = (f32[32,256]{1,0:T(8,128)S(1)}, f32[32,256]{1,0:T(8,128)}, u32[]{:S(2)}) copy-start(f32[32,256]{1,0:T(8,128)} %reduce-scatter.15.cloned.1.call-done) | copy-start | bytes 98308
  1458.4 304.3 %all-reduce.18.cloned.1.call-start = ((), (), s32[]{:S(2)}) async-start(), calls=%async_computation.17 | async-start | bytes 524288 | tf_op jit(solution)/shard_map/psum | solution.py:12
  1593.7 265.5 %reduce-scatter.19.cloned.1.call-start = ((), (), s32[]{:S(2)}) async-start(), calls=%async_computation.18 | async-start | bytes 557056 | tf_op jit(solution)/shard_map/reduce_scatter | solution.py:48
  1764.9 304.3 %all-reduce.20.cloned.1.call-start = ((), (), s32[]{:S(2)}) async-start(), calls=%async_computation.19 | async-start | bytes 524288 | tf_op jit(solution)/shard_map/psum | solution.py:12
  1900.1 265.5 %reduce-scatter.21.cloned.1.call-start = ((), (), s32[]{:S(2)}) async-start(), calls=%async_computation.20 | async-start | bytes 557056 | tf_op jit(solution)/shard_map/reduce_scatter | solution.py:48
  2071.3 94.3 %copy-start.4 = (f32[32,256]{1,0:T(8,128)S(1)}, f32[32,256]{1,0:T(8,128)}, u32[]{:S(2)}) copy-start(f32[32,256]{1,0:T(8,128)} %reduce-scatter.19.cloned.1.call-done) | copy-start | bytes 98308
  2071.3 304.3 %all-reduce.22.cloned.1.call-start = ((), (), s32[]{:S(2)}) async-start(), calls=%async_computation.21 | async-start | bytes 524288 | tf_op jit(solution)/shard_map/psum | solution.py:12
  2206.6 265.4 %reduce-scatter.23.cloned.1.call-start = ((), (), s32[]{:S(2)}) async-start(), calls=%async_computation.22 | async-start | bytes 557056 | tf_op jit(solution)/shard_map/reduce_scatter | solution.py:48
  2377.7 94.2 %copy-start.6 = (f32[32,256]{1,0:T(8,128)S(1)}, f32[32,256]{1,0:T(8,128)}, u32[]{:S(2)}) copy-start(f32[32,256]{1,0:T(8,128)} %reduce-scatter.21.cloned.1.call-done) | copy-start | bytes 98308
Sparse Core Ops, SparseCore 0:
  55.3 171.9 all-reduce.23
  232.2 93.9 reduce-scatter.8
  367.0 169.5 all-reduce.9
  538.9 93.9 reduce-scatter.10
  674.1 168.9 all-reduce.11
  845.4 93.9 reduce-scatter.12
  980.5 168.9 all-reduce.13
  1152.0 94.0 reduce-scatter.14
  1287.2 169.1 all-reduce.15
  1458.7 93.9 reduce-scatter.16
  1593.8 168.9 all-reduce.17
  1765.1 93.9 reduce-scatter.18
  1900.3 168.9 all-reduce.19
  2071.6 93.9 reduce-scatter.20
  2206.7 168.9 all-reduce.21
  2378.0 93.9 reduce-scatter.22
where the time goes:
time: 2480 us
  waiting for transfers between devices  2110 us (85%)
  blocking collectives  322 us (13%)
    psum x8, waiting for transfers between devices, broadcast(): return lax.psum(kept, axis)  1360 us
    reduce_scatter x8, waiting for transfers between devices, body(): lax.psum_scatter(partial_value, 'col', scatter_dimension=0, tiled=True)  754 us
    all_gather x8, blocking collectives, body(): gathered = lax.all_gather(squashed, 'col', axis=0, tiled=True)  322 us
  transfers between devices with their start and end apart: 16, of which 16 were waited for; matrix products, arithmetic and copies ran while one was open for 0% of the time, Pallas kernels for 0%

commit v1 on v0

--- a/solution.py
+++ b/solution.py
@@ -9,7 +9,7 @@
 
 def broadcast(value, axis, source):
     kept = jnp.where(lax.axis_index(axis) == source, value, 0).astype(value.dtype)
-    return lax.psum(kept, axis)
+    return jnp.sum(lax.all_gather(kept, axis), axis=0)
 
 
 def spread(panel, root):

time: 2480 us -> 1860 us (0.75)
  waiting for transfers between devices: 2110 us -> 1460 us
  other arithmetic: 14.5 us -> 47.7 us
    psum x8 -> x0, waiting for transfers between devices: 1360 us -> none  [broadcast(): return lax.psum(kept, axis)]
    all_gather x0 -> x10, waiting for transfers between devices: none -> 803 us  [broadcast(): return jnp.sum(lax.all_gather(kept, axis), axis=0)]
    reduce_scatter x8, waiting for transfers between devices: 754 us -> 655 us  [body(): lax.psum_scatter(partial_value, 'col', scatter_dimension=0, tiled=True)]
    reduce_sum x0 -> x10, other arithmetic: none -> 32.4 us  [broadcast(): return jnp.sum(lax.all_gather(kept, axis), axis=0)]
  transfers between devices with their start and end apart: 16 -> 18, of which waited for: 16 -> 18; matrix products, arithmetic and copies ran while one was open for 0% -> 1% of each run, Pallas kernels for 0% -> 0%
where the time goes in v1:
time: 1860 us; the launch traced here: 1850 us
  waiting for transfers between devices  1460 us (78%)
  blocking collectives  322 us (17%)
  other arithmetic  47.7 us (3%)
    all_gather x10, waiting for transfers between devices, broadcast(): return jnp.sum(lax.all_gather(kept, axis), axis=0)  803 us
    reduce_scatter x8, waiting for transfers between devices, body(): lax.psum_scatter(partial_value, 'col', scatter_dimension=0, tiled=True)  655 us
    all_gather x8, blocking collectives, body(): gathered = lax.all_gather(squashed, 'col', axis=0, tiled=True)  322 us
  transfers between devices with their start and end apart: 18, of which 18 were waited for; matrix products, arithmetic and copies ran while one was open for 1% of the time, Pallas kernels for 0%

profile of v1, /device:TPU:8, one launch (start us, length us, event | category | flops | bytes accessed | tf_op | source)
XLA Modules:
  0.0 1854.4 jit_solution(10379672264522985195)
XLA Ops:
  7.3 46.0 %all_gather.88 = bf16[512,256]{1,0:T(8,128)(2,1)S(1)} all-gather(bf16[32,256]{1,0:T(8,128)(2,1)S(1)} %tanh_convert_fusion.7), channel_id=1, replica_groups=mesh['row'=16,'col'=16] {'col'}, dimensions={0}, use_global_device_ids=true | all-gather | bytes 278528 | tf_op jit(solution)/shard_map/all_gather | solution.py:45
  55.9 72.7 %all-gather.25.cloned.1.call-done = bf16[8192,256]{1,0:T(8,128)(2,1)} async-done(((bf16[512,256]{1,0:T(8,128)(2,1)}), bf16[8192,256]{1,0:T(8,128)(2,1)}) %all-gather.25.cloned.1.call-update) | async-done | bytes 4194320 | tf_op jit(solution)/shard_map/all_gather | solution.py:12
  128.6 2.9 reduce_sum.122
  131.5 102.9 %all-gather.21.cloned.1.call-done = bf16[32,512,256]{2,1,0:T(8,128)(2,1)} async-done(((bf16[2,512,256]{2,1,0:T(8,128)(2,1)}), bf16[32,512,256]{2,1,0:T(8,128)(2,1)}) %all-gather.21.cloned.1.call-update) | async-done | bytes 8388624 | tf_op jit(solution)/shard_map/all_gather | solution.py:12
  234.4 4.8 reduce_sum.120
  239.9 100.1 %all-gather.23.cloned.1.call-done = bf16[32,512,256]{2,1,0:T(8,128)(2,1)} async-done(((bf16[2,512,256]{2,1,0:T(8,128)(2,1)}), bf16[32,512,256]{2,1,0:T(8,128)(2,1)}) %all-gather.23.cloned.1.call-update) | async-done | bytes 8388624 | tf_op jit(solution)/shard_map/all_gather | solution.py:12
  340.0 4.8 reduce_sum.121
  347.7 81.6 %reduce-scatter.9.cloned.1.call-done = f32[32,256]{1,0:T(8,128)} async-done(((f32[512,256]{1,0:T(8,128)}), f32[32,256]{1,0:T(8,128)}) %reduce-scatter.9.cloned.1.call-update) | async-done | bytes 32784 | tf_op jit(solution)/shard_map/reduce_scatter | solution.py:48
  430.1 39.5 %all_gather.91 = bf16[512,256]{1,0:T(8,128)(2,1)S(1)} all-gather(bf16[32,256]{1,0:T(8,128)(2,1)S(1)} %get-tuple-element.9), channel_id=1, replica_groups=mesh['row'=16,'col'=16] {'col'}, dimensions={0}, use_global_device_ids=true | all-gather | bytes 278528 | tf_op jit(solution)/shard_map/all_gather | solution.py:45
  470.4 75.4 %all-gather.27.cloned.1.call-done = bf16[8192,256]{1,0:T(8,128)(2,1)} async-done(((bf16[512,256]{1,0:T(8,128)(2,1)}), bf16[8192,256]{1,0:T(8,128)(2,1)}) %all-gather.27.cloned.1.call-update) | async-done | bytes 4194320 | tf_op jit(solution)/shard_map/all_gather | solution.py:12
  545.8 2.9 reduce_sum.123
  549.9 81.9 %reduce-scatter.11.cloned.1.call-done = f32[32,256]{1,0:T(8,128)} async-done(((f32[512,256]{1,0:T(8,128)}), f32[32,256]{1,0:T(8,128)}) %reduce-scatter.11.cloned.1.call-update) | async-done | bytes 32784 | tf_op jit(solution)/shard_map/reduce_scatter | solution.py:48
  632.6 39.5 %all_gather.94 = bf16[512,256]{1,0:T(8,128)(2,1)S(1)} all-gather(bf16[32,256]{1,0:T(8,128)(2,1)S(1)} %tanh_convert_fusion.5), channel_id=1, replica_groups=mesh['row'=16,'col'=16] {'col'}, dimensions={0}, use_global_device_ids=true | all-gather | bytes 278528 | tf_op jit(solution)/shard_map/all_gather | solution.py:45
  672.9 75.2 %all-gather.29.cloned.1.call-done = bf16[8192,256]{1,0:T(8,128)(2,1)} async-done(((bf16[512,256]{1,0:T(8,128)(2,1)}), bf16[8192,256]{1,0:T(8,128)(2,1)}) %all-gather.29.cloned.1.call-update) | async-done | bytes 4194320 | tf_op jit(solution)/shard_map/all_gather | solution.py:12
  748.2 2.9 reduce_sum.124
  752.3 82.0 %reduce-scatter.13.cloned.1.call-done = f32[32,256]{1,0:T(8,128)} async-done(((f32[512,256]{1,0:T(8,128)}), f32[32,256]{1,0:T(8,128)}) %reduce-scatter.13.cloned.1.call-update) | async-done | bytes 32784 | tf_op jit(solution)/shard_map/reduce_scatter | solution.py:48
  835.0 39.3 %all_gather.97 = bf16[512,256]{1,0:T(8,128)(2,1)S(1)} all-gather(bf16[32,256]{1,0:T(8,128)(2,1)S(1)} %get-tuple-element.7), channel_id=1, replica_groups=mesh['row'=16,'col'=16] {'col'}, dimensions={0}, use_global_device_ids=true | all-gather | bytes 278528 | tf_op jit(solution)/shard_map/all_gather | solution.py:45
  875.1 75.3 %all-gather.31.cloned.1.call-done = bf16[8192,256]{1,0:T(8,128)(2,1)} async-done(((bf16[512,256]{1,0:T(8,128)(2,1)}), bf16[8192,256]{1,0:T(8,128)(2,1)}) %all-gather.31.cloned.1.call-update) | async-done | bytes 4194320 | tf_op jit(solution)/shard_map/all_gather | solution.py:12
  950.4 2.9 reduce_sum.125
  954.5 81.9 %reduce-scatter.15.cloned.1.call-done = f32[32,256]{1,0:T(8,128)} async-done(((f32[512,256]{1,0:T(8,128)}), f32[32,256]{1,0:T(8,128)}) %reduce-scatter.15.cloned.1.call-update) | async-done | bytes 32784 | tf_op jit(solution)/shard_map/reduce_scatter | solution.py:48
  1037.2 39.3 %all_gather.100 = bf16[512,256]{1,0:T(8,128)(2,1)S(1)} all-gather(bf16[32,256]{1,0:T(8,128)(2,1)S(1)} %tanh_convert_fusion.3), channel_id=1, replica_groups=mesh['row'=16,'col'=16] {'col'}, dimensions={0}, use_global_device_ids=true | all-gather | bytes 278528 | tf_op jit(solution)/shard_map/all_gather | solution.py:45
  1077.3 75.6 %all-gather.33.cloned.1.call-done = bf16[8192,256]{1,0:T(8,128)(2,1)} async-done(((bf16[512,256]{1,0:T(8,128)(2,1)}), bf16[8192,256]{1,0:T(8,128)(2,1)}) %all-gather.33.cloned.1.call-update) | async-done | bytes 4194320 | tf_op jit(solution)/shard_map/all_gather | solution.py:12
  1157.0 81.9 %reduce-scatter.17.cloned.1.call-done = f32[32,256]{1,0:T(8,128)} async-done(((f32[512,256]{1,0:T(8,128)}), f32[32,256]{1,0:T(8,128)}) %reduce-scatter.17.cloned.1.call-update) | async-done | bytes 32784 | tf_op jit(solution)/shard_map/reduce_scatter | solution.py:48
  1239.6 39.6 %all_gather.103 = bf16[512,256]{1,0:T(8,128)(2,1)S(1)} all-gather(bf16[32,256]{1,0:T(8,128)(2,1)S(1)} %get-tuple-element.5), channel_id=1, replica_groups=mesh['row'=16,'col'=16] {'col'}, dimensions={0}, use_global_device_ids=true | all-gather | bytes 278528 | tf_op jit(solution)/shard_map/all_gather | solution.py:45
  1280.0 75.2 %all-gather.35.cloned.1.call-done = bf16[8192,256]{1,0:T(8,128)(2,1)} async-done(((bf16[512,256]{1,0:T(8,128)(2,1)}), bf16[8192,256]{1,0:T(8,128)(2,1)}) %all-gather.35.cloned.1.call-update) | async-done | bytes 4194320 | tf_op jit(solution)/shard_map/all_gather | solution.py:12
  1359.2 81.8 %reduce-scatter.19.cloned.1.call-done = f32[32,256]{1,0:T(8,128)} async-done(((f32[512,256]{1,0:T(8,128)}), f32[32,256]{1,0:T(8,128)}) %reduce-scatter.19.cloned.1.call-update) | async-done | bytes 32784 | tf_op jit(solution)/shard_map/reduce_scatter | solution.py:48
  1441.9 39.7 %all_gather.106 = bf16[512,256]{1,0:T(8,128)(2,1)S(1)} all-gather(bf16[32,256]{1,0:T(8,128)(2,1)S(1)} %tanh_convert_fusion.1), channel_id=1, replica_groups=mesh['row'=16,'col'=16] {'col'}, dimensions={0}, use_global_device_ids=true | all-gather | bytes 278528 | tf_op jit(solution)/shard_map/all_gather | solution.py:45
  1482.4 75.4 %all-gather.37.cloned.1.call-done = bf16[8192,256]{1,0:T(8,128)(2,1)} async-done(((bf16[512,256]{1,0:T(8,128)(2,1)}), bf16[8192,256]{1,0:T(8,128)(2,1)}) %all-gather.37.cloned.1.call-update) | async-done | bytes 4194320 | tf_op jit(solution)/shard_map/all_gather | solution.py:12
  1561.8 81.9 %reduce-scatter.21.cloned.1.call-done = f32[32,256]{1,0:T(8,128)} async-done(((f32[512,256]{1,0:T(8,128)}), f32[32,256]{1,0:T(8,128)}) %reduce-scatter.21.cloned.1.call-update) | async-done | bytes 32784 | tf_op jit(solution)/shard_map/reduce_scatter | solution.py:48
  1644.6 39.3 %all_gather.109 = bf16[512,256]{1,0:T(8,128)(2,1)S(1)} all-gather(bf16[32,256]{1,0:T(8,128)(2,1)S(1)} %tanh_convert_fusion), channel_id=1, replica_groups=mesh['row'=16,'col'=16] {'col'}, dimensions={0}, use_global_device_ids=true | all-gather | bytes 278528 | tf_op jit(solution)/shard_map/all_gather | solution.py:45
  1684.7 75.6 %all-gather.39.cloned.1.call-done = bf16[8192,256]{1,0:T(8,128)(2,1)} async-done(((bf16[512,256]{1,0:T(8,128)(2,1)}), bf16[8192,256]{1,0:T(8,128)(2,1)}) %all-gather.39.cloned.1.call-update) | async-done | bytes 4194320 | tf_op jit(solution)/shard_map/all_gather | solution.py:12
  1764.3 81.8 %reduce-scatter.23.cloned.1.call-done = f32[32,256]{1,0:T(8,128)} async-done(((f32[512,256]{1,0:T(8,128)}), f32[32,256]{1,0:T(8,128)}) %reduce-scatter.23.cloned.1.call-update) | async-done | bytes 32784 | tf_op jit(solution)/shard_map/reduce_scatter | solution.py:48
  (83 shorter events, 39.1 us)
Async XLA Ops:
  6.5 122.1 %all-gather.25.cloned.1.call-start = ((), (), s32[]{:S(2)}) async-start(), calls=%async_computation.18 | async-start | bytes 4456448 | tf_op jit(solution)/shard_map/all_gather | solution.py:12
  54.0 180.4 %all-gather.21.cloned.1.call-start = ((), (), s32[]{:S(2)}) async-start(), calls=%async_computation.16 | async-start | bytes 8912896 | tf_op jit(solution)/shard_map/all_gather | solution.py:12
  55.0 285.1 %all-gather.23.cloned.1.call-start = ((), (), s32[]{:S(2)}) async-start(), calls=%async_computation.17 | async-start | bytes 8912896 | tf_op jit(solution)/shard_map/all_gather | solution.py:12
  55.9 373.4 %reduce-scatter.9.cloned.1.call-start = ((), (), s32[]{:S(2)}) async-start(), calls=%async_computation.8 | async-start | bytes 557056 | tf_op jit(solution)/shard_map/reduce_scatter | solution.py:48
  234.4 4.8 copy-start.1
  340.0 4.8 copy-start
  347.6 198.2 %all-gather.27.cloned.1.call-start = ((), (), s32[]{:S(2)}) async-start(), calls=%async_computation.19 | async-start | bytes 4456448 | tf_op jit(solution)/shard_map/all_gather | solution.py:12
  470.3 161.4 %reduce-scatter.11.cloned.1.call-start = ((), (), s32[]{:S(2)}) async-start(), calls=%async_computation.9 | async-start | bytes 557056 | tf_op jit(solution)/shard_map/reduce_scatter | solution.py:48
  549.8 198.3 %all-gather.29.cloned.1.call-start = ((), (), s32[]{:S(2)}) async-start(), calls=%async_computation.20 | async-start | bytes 4456448 | tf_op jit(solution)/shard_map/all_gather | solution.py:12
  631.8 202.5 %copy-start.4 = (f32[32,256]{1,0:T(8,128)S(1)}, f32[32,256]{1,0:T(8,128)}, u32[]{:S(2)}) copy-start(f32[32,256]{1,0:T(8,128)} %reduce-scatter.11.cloned.1.call-done) | copy-start | bytes 98308
  672.9 161.3 %reduce-scatter.13.cloned.1.call-start = ((), (), s32[]{:S(2)}) async-start(), calls=%async_computation.10 | async-start | bytes 557056 | tf_op jit(solution)/shard_map/reduce_scatter | solution.py:48
  752.2 198.2 %all-gather.31.cloned.1.call-start = ((), (), s32[]{:S(2)}) async-start(), calls=%async_computation.21 | async-start | bytes 4456448 | tf_op jit(solution)/shard_map/all_gather | solution.py:12
  875.1 161.3 %reduce-scatter.15.cloned.1.call-start = ((), (), s32[]{:S(2)}) async-start(), calls=%async_computation.11 | async-start | bytes 557056 | tf_op jit(solution)/shard_map/reduce_scatter | solution.py:48
  954.4 198.5 %all-gather.33.cloned.1.call-start = ((), (), s32[]{:S(2)}) async-start(), calls=%async_computation.22 | async-start | bytes 4456448 | tf_op jit(solution)/shard_map/all_gather | solution.py:12
  1036.4 202.5 %copy-start.5 = (f32[32,256]{1,0:T(8,128)S(1)}, f32[32,256]{1,0:T(8,128)}, u32[]{:S(2)}) copy-start(f32[32,256]{1,0:T(8,128)} %reduce-scatter.15.cloned.1.call-done) | copy-start | bytes 98308
  1077.3 161.6 %reduce-scatter.17.cloned.1.call-start = ((), (), s32[]{:S(2)}) async-start(), calls=%async_computation.12 | async-start | bytes 557056 | tf_op jit(solution)/shard_map/reduce_scatter | solution.py:48
  1156.9 198.2 %all-gather.35.cloned.1.call-start = ((), (), s32[]{:S(2)}) async-start(), calls=%async_computation.23 | async-start | bytes 4456448 | tf_op jit(solution)/shard_map/all_gather | solution.py:12
  1279.9 161.1 %reduce-scatter.19.cloned.1.call-start = ((), (), s32[]{:S(2)}) async-start(), calls=%async_computation.13 | async-start | bytes 557056 | tf_op jit(solution)/shard_map/reduce_scatter | solution.py:48
  1359.2 198.6 %all-gather.37.cloned.1.call-start = ((), (), s32[]{:S(2)}) async-start(), calls=%async_computation.24 | async-start | bytes 4456448 | tf_op jit(solution)/shard_map/all_gather | solution.py:12
  1441.0 202.7 %copy-start.2 = (f32[32,256]{1,0:T(8,128)S(1)}, f32[32,256]{1,0:T(8,128)}, u32[]{:S(2)}) copy-start(f32[32,256]{1,0:T(8,128)} %reduce-scatter.19.cloned.1.call-done) | copy-start | bytes 98308
  1482.3 161.4 %reduce-scatter.21.cloned.1.call-start = ((), (), s32[]{:S(2)}) async-start(), calls=%async_computation.14 | async-start | bytes 557056 | tf_op jit(solution)/shard_map/reduce_scatter | solution.py:48
  1561.8 198.6 %all-gather.39.cloned.1.call-start = ((), (), s32[]{:S(2)}) async-start(), calls=%async_computation.25 | async-start | bytes 4456448 | tf_op jit(solution)/shard_map/all_gather | solution.py:12
  1643.7 202.5 %copy-start.3 = (f32[32,256]{1,0:T(8,128)S(1)}, f32[32,256]{1,0:T(8,128)}, u32[]{:S(2)}) copy-start(f32[32,256]{1,0:T(8,128)} %reduce-scatter.21.cloned.1.call-done) | copy-start | bytes 98308
  1684.6 161.5 %reduce-scatter.23.cloned.1.call-start = ((), (), s32[]{:S(2)}) async-start(), calls=%async_computation.15 | async-start | bytes 557056 | tf_op jit(solution)/shard_map/reduce_scatter | solution.py:48
Sparse Core Ops, SparseCore 0:
  54.2 74.4 all-gather.24
  131.3 103.0 all-gather.20
  237.1 102.8 all-gather.22
  347.7 81.5 reduce-scatter.8
  470.5 75.3 all-gather.26
  550.0 81.7 reduce-scatter.10
  673.0 75.1 all-gather.28
  752.3 81.8 reduce-scatter.12
  875.2 75.1 all-gather.30
  954.5 81.7 reduce-scatter.14
  1077.4 75.4 all-gather.32
  1157.0 81.7 reduce-scatter.16
  1280.0 75.0 all-gather.34
  1359.3 81.6 reduce-scatter.18
  1482.4 75.2 all-gather.36
  1561.9 81.7 reduce-scatter.20
  1684.7 75.5 all-gather.38
  1764.4 81.6 reduce-scatter.22
